TPU v7x, 32 devices: a whole 2x2x4 slice. The times are simulated.
32 devices in a mesh: dp: 8 (over y, x, core), tensor: 4 (over z).
Axes of the slice: x: 2, y: 2, z: 4, core: 2. Of those that a mesh axis runs over, the one named last changes fastest.
Arguments:
- activations: bfloat16 [4096, 4096], P('dp'), may hold values from -1000 to 1000
- norm_gain: bfloat16 [4096], replicated, may hold values from 0.5 to 1.5
- query_blocks: bfloat16 [128, 32, 4096], P('dp', None, 'tensor'), may hold values from -64 to 64
- query_scales: int32 [128, 1, 4096], P('dp', None, 'tensor'), may hold values from -9 to -5
- key_blocks: bfloat16 [128, 32, 512], P('dp', None, 'tensor'), may hold values from -64 to 64
- key_scales: int32 [128, 1, 512], P('dp', None, 'tensor'), may hold values from -9 to -5
- value_blocks: bfloat16 [128, 32, 512], P('dp', None, 'tensor'), may hold values from -6 to 6
- value_scales: int32 [128, 1, 512], P('dp', None, 'tensor'), may hold values from -9 to -5
- output_blocks: bfloat16 [128, 32, 4096], P('tensor', None, 'dp'), may hold values from -6 to 6
- output_scales: int32 [128, 1, 4096], P('tensor', None, 'dp'), may hold values from -9 to -5
Outputs:
- attended: bfloat16 [4096, 4096], P('dp')
All inputs are finite; a program needn't handle non-finite values.
Results may differ from a plain program's by a relative error of at most 0.015.
The roundings to bfloat16 on the way count: a program that leaves them out, or rounds other values in their place, can miss the bound.
Values may be sent and summed in bfloat16 or wider, within the bound.
No kernel may reach another device: no remote copies, remote signals or barrier semaphores. Data moves between devices by JAX's collectives and lax.ppermute only.
A program may use at most 128 MiB of HBM per device.

v0:
```python
import math
import jax
import jax.numpy as jnp
from jax import lax
from jax.sharding import PartitionSpec as P

HEAD_DIM = 128
SEQ = 256
EPS = 1e-05
ROPE_BASE = 500000.0


def dequant(blocks, scales):
    factor = jnp.exp2(scales.astype(jnp.float32)).astype(blocks.dtype)
    weight = blocks * factor
    return weight.reshape(weight.shape[0] * weight.shape[1], weight.shape[2])


def rotate_pairs(states, positions):
    half_dim = states.shape[-1] // 2
    frequency = jnp.exp(
        -math.log(ROPE_BASE) * jnp.arange(half_dim, dtype=jnp.float32) * 2.0 / states.shape[-1]
    )
    angles = positions.astype(jnp.float32)[:, None] * frequency[None, :]
    cosine = jnp.cos(angles)[None, :, None, :]
    sine_part = jnp.sin(angles)[None, :, None, :]
    first = states[..., :half_dim]
    second = states[..., half_dim:]
    return jnp.concatenate(
        [first * cosine - second * sine_part, second * cosine + first * sine_part], axis=-1
    )


def attend(query_states, key_states, value_states, kv_count):
    tokens_here = query_states.shape[0]
    count = tokens_here // SEQ
    positions = jnp.arange(SEQ, dtype=jnp.int32)
    queries = rotate_pairs(query_states.reshape(count, SEQ, -1, HEAD_DIM), positions).astype(
        jnp.bfloat16
    )
    rotated_keys = rotate_pairs(
        key_states.reshape(count, SEQ, kv_count, HEAD_DIM), positions
    ).astype(jnp.bfloat16)
    value_heads = value_states.astype(jnp.bfloat16).reshape(count, SEQ, kv_count, HEAD_DIM)
    group_size = queries.shape[2] // kv_count
    queries = queries.reshape(count, SEQ, kv_count, group_size, HEAD_DIM)
    scores = jnp.einsum(
        "sqkgd,stkd->skgqt", queries, rotated_keys, preferred_element_type=jnp.float32
    ) * HEAD_DIM ** (-0.5)
    visible = positions[:, None] >= positions[None, :]
    scores = jnp.where(visible, scores, -jnp.inf)
    attn_weights = jax.nn.softmax(scores, axis=-1).astype(jnp.bfloat16)
    context = jnp.einsum(
        "skgqt,stkd->sqkgd", attn_weights, value_heads, preferred_element_type=jnp.float32
    )
    return context.astype(jnp.bfloat16).reshape(tokens_here, -1)


def shards(
    activations,
    norm_gain,
    query_blocks,
    query_scales,
    key_blocks,
    key_scales,
    value_blocks,
    value_scales,
    output_blocks,
    output_scales,
):
    query_exps = query_scales.astype(jnp.bfloat16)
    key_exps = key_scales.astype(jnp.bfloat16)
    value_exps = value_scales.astype(jnp.bfloat16)
    output_exps = output_scales.astype(jnp.bfloat16)
    wide_rows = activations.astype(jnp.float32)
    inverse = lax.rsqrt(jnp.mean(wide_rows * wide_rows, axis=-1, keepdims=True) + EPS)
    normed = (wide_rows * inverse * norm_gain.astype(jnp.float32)).astype(jnp.bfloat16)

    def product(blocks, scales):
        return jnp.dot(normed, dequant(blocks, scales), preferred_element_type=jnp.float32)

    def add_one(pieces):
        return product(pieces[0], pieces[1])

    query_states = add_one(
        (
            lax.all_gather(query_blocks, "dp", axis=0, tiled=True),
            lax.all_gather(query_exps, "dp", axis=0, tiled=True),
        )
    )
    key_states = add_one(
        (
            lax.all_gather(key_blocks, "dp", axis=0, tiled=True),
            lax.all_gather(key_exps, "dp", axis=0, tiled=True),
        )
    )
    value_states = add_one(
        (
            lax.all_gather(value_blocks, "dp", axis=0, tiled=True),
            lax.all_gather(value_exps, "dp", axis=0, tiled=True),
        )
    )
    context = attend(query_states, key_states, value_states, key_blocks.shape[2] // HEAD_DIM)
    pieces = (
        lax.all_gather(output_blocks, "dp", axis=2, tiled=True),
        lax.all_gather(output_exps, "dp", axis=2, tiled=True),
    )
    block_out = jnp.dot(context, dequant(pieces[0], pieces[1]), preferred_element_type=jnp.float32)
    return lax.psum(block_out.astype(jnp.bfloat16), "tensor")


def solution(mesh):
    placed = (
        P("dp", None),
        P(),
        P("dp", None, "tensor"),
        P("dp", None, "tensor"),
        P("dp", None, "tensor"),
        P("dp", None, "tensor"),
        P("dp", None, "tensor"),
        P("dp", None, "tensor"),
        P("tensor", None, "dp"),
        P("tensor", None, "dp"),
    )
    return jax.shard_map(
        shards, mesh=mesh, in_specs=placed, out_specs=P("dp", None), check_vma=False
    )
```

profile of v0, /device:TPU:0, one launch (start us, length us, event | category | flops | bytes accessed | tf_op | source)
XLA Modules:
  0.0 358.5 jit_solution(17838992438456256269)
XLA Ops:
  6.5 0.0 copy-start.1
  6.5 0.0 all-gather.7.cloned.1.call-start
  6.5 0.7 all-gather.7.cloned.1.call-update
  7.3 0.0 all-gather.5.cloned.1.call-start
  7.3 0.7 all-gather.5.cloned.1.call-update
  8.0 0.0 all-gather.9.cloned.1.call-start
  8.1 0.7 all-gather.9.cloned.1.call-update
  8.7 0.0 all-gather.11.cloned.1.call-start
  8.8 0.5 all-gather.11.cloned.1.call-update
  9.3 0.0 all-reduce.2.cloned.1.call-start
  9.4 0.0 copy-start
  9.4 0.9 convert_element_type.93
  10.2 0.9 convert_element_type.99
  11.1 0.7 convert_element_type.95
  11.8 0.9 convert_element_type.110
  12.7 12.4 %all_gather.31 = bf16[32,1,4096]{2,1,0:T(2,128)(2,1)S(1)} all-gather(bf16[32,1,512]{2,1,0:T(2,128)(2,1)S(1)} %convert_element_type.110), channel_id=1, replica_groups=mesh['dp'=8,'tensor'=4] {'dp'}, dimensions={2}, use_global_device_ids=true | all-gather | bytes 294912 | tf_op jit(solution)/shard_map/all_gather | solution.py:106
  25.1 0.9 exponential_convert_fusion
  26.1 0.3 copy.53
  26.4 9.1 %all_gather.27 = bf16[128,1,128]{2,0,1:T(8,128)(2,1)S(1)} all-gather(bf16[16,1,128]{2,0,1:T(8,128)(2,1)S(1)} %convert_element_type.99), channel_id=1, replica_groups=mesh['dp'=8,'tensor'=4] {'dp'}, dimensions={0}, use_global_device_ids=true | all-gather | bytes 36864 | tf_op jit(solution)/shard_map/all_gather | solution.py:94
  35.5 8.3 %all_gather.25 = bf16[128,1,128]{2,0,1:T(8,128)(2,1)S(1)} all-gather(bf16[16,1,128]{2,0,1:T(8,128)(2,1)S(1)} %convert_element_type.95), channel_id=1, replica_groups=mesh['dp'=8,'tensor'=4] {'dp'}, dimensions={0}, use_global_device_ids=true | all-gather | bytes 36864 | tf_op jit(solution)/shard_map/all_gather | solution.py:100
  43.8 0.0 copy-done.1
  43.8 9.4 %all_gather.29 = bf16[128,1,1024]{2,0,1:T(8,128)(2,1)S(1)} all-gather(bf16[16,1,1024]{2,0,1:T(8,128)(2,1)S(1)} %copy_convert_fusion), channel_id=1, replica_groups=mesh['dp'=8,'tensor'=4] {'dp'}, dimensions={0}, use_global_device_ids=true | all-gather | bytes 294912 | tf_op jit(solution)/shard_map/all_gather | solution.py:88
  53.2 3.1 fusion
  56.4 0.3 multiply_cosine_fusion
  56.7 0.1 fusion.20
  56.8 0.0 copy-done
  56.8 3.6 %fusion.2 = bf16[512,4096]{1,0:T(8,128)(2,1)} fusion(bf16[512,4096]{1,0:T(8,128)(2,1)S(1)} %copy-done, f32[4096]{0:T(1024)S(1)} %convert_element_type.93, f32[512]{0:T(512)S(1)} %add_rsqrt_fusion), kind=kLoop, calls=%fused_computation.4 | loop fusion | flops 8388608 | bytes 8407040 | tf_op jit(solution)/shard_map/convert_element_type | solution.py:77
  60.4 0.0 all-gather.7.cloned.1.call-done
  60.4 1.3 broadcast_multiply_fusion.2
  61.8 3.7 %convolution_bitcast_fusion = f32[2,256,1,128]{1,3,0,2:T(8,128)S(1)} fusion(bf16[2,256,4096]{2,1,0:T(8,128)(2,1)} %bitcast.88, bf16[4096,128,1]{1,0,2:T(8,128)(2,1)S(1)} %bitcast.92), kind=kOutput, calls=%fused_computation.18 | convolution fusion | flops 536870912 | bytes 5505024 | tf_op jit(solution)/shard_map/dot_general | solution.py:80
  65.5 0.0 all-gather.5.cloned.1.call-done
  65.5 1.3 broadcast_multiply_fusion.3
  66.8 3.4 convolution_convert_fusion.1
  70.3 47.6 %all-gather.9.cloned.1.call-done = bf16[128,32,1024]{2,1,0:T(8,128)(2,1)} async-done(((bf16[16,32,1024]{2,1,0:T(8,128)(2,1)}), bf16[128,32,1024]{2,1,0:T(8,128)(2,1)}) %all-gather.9.cloned.1.call-update) | async-done | bytes 8388624 | tf_op jit(solution)/shard_map/all_gather | solution.py:87
  117.9 7.2 %broadcast_multiply_fusion.1 = bf16[128,32,1024]{2,1,0:T(8,128)(2,1)} fusion(bf16[128,32,1024]{2,1,0:T(8,128)(2,1)} %all-gather.9.cloned.1.call-done, bf16[128,1024]{1,0:T(8,128)(2,1)S(1)} %fusion.20), kind=kLoop, calls=%fused_computation.10 | loop fusion | flops 4194304 | bytes 17039360 | tf_op jit(solution)/shard_map/mul | solution.py:15
  125.1 12.1 %copy.28 = bf16[1024,4096]{1,0:T(8,128)(2,1)} copy(bf16[1024,4096]{0,1:T(8,128)(2,1)} %bitcast.87) | data formatting | bytes 16777216 | tf_op jit(solution)/shard_map/dot_general | solution.py:80
  137.2 8.2 %fusion.30 = f32[2,256,8,128]{1,3,2,0:T(8,128)S(1)} fusion(bf16[2,256,4096,1]{2,1,3,0:T(8,128)(2,1)} %bitcast.89, bf16[8,128,4096,1]{2,1,0,3:T(8,128)(2,1)} %bitcast.91), kind=kOutput, calls=%fused_computation.55 | convolution fusion | flops 4294967296 | bytes 14680064 | tf_op jit(solution)/shard_map/dot_general | solution.py:80
  145.4 0.3 subtract_convert_fusion
  145.8 0.8 fusion.4
  146.6 0.9 fusion.3
  147.5 1.3 fusion.11
  148.8 0.8 copy.33
  149.5 26.0 %all-gather.11.cloned.1.call-done = bf16[32,32,4096]{2,1,0:T(8,128)(2,1)} async-done(((bf16[32,32,512]{2,1,0:T(8,128)(2,1)}), bf16[32,32,4096]{2,1,0:T(8,128)(2,1)}) %all-gather.11.cloned.1.call-update) | async-done | bytes 8388624 | tf_op jit(solution)/shard_map/all_gather | solution.py:105
  175.5 7.3 %broadcast_multiply_fusion = bf16[32,32,4096]{2,1,0:T(8,128)(2,1)} fusion(bf16[32,32,4096]{2,1,0:T(8,128)(2,1)} %all-gather.11.cloned.1.call-done, bf16[32,4096]{1,0:T(8,128)(2,1)S(1)} %bitcast.93), kind=kLoop, calls=%fused_computation.7 | loop fusion | flops 4194304 | bytes 17039360 | tf_op jit(solution)/shard_map/mul | solution.py:15
  182.8 9.4 %convolution_convert_fusion = bf16[512,4096]{1,0:T(8,128)(2,1)} fusion(bf16[1024,4096]{1,0:T(8,128)(2,1)} %bitcast.90, bf16[64,8,8,128]{3,2,1,0:T(8,128)(2,1)S(1)} %bitcast.94), kind=kOutput, calls=%fused_computation.5 | convolution fusion | flops 4297064448 | bytes 13631488 | tf_op jit(solution)/shard_map/dot_general | solution.py:108
  192.2 0.0 all-reduce.2.cloned.1.call-update
  192.2 155.1 %all-reduce.2.cloned.1.call-done = bf16[512,4096]{1,0:T(8,128)(2,1)} async-done(((bf16[512,4096]{1,0:T(8,128)(2,1)}), bf16[512,4096]{1,0:T(8,128)(2,1)}) %all-reduce.2.cloned.1.call-update) | async-done | bytes 4194320 | tf_op jit(solution)/shard_map/psum | solution.py:109
  347.3 4.7 %copy.55 = bf16[512,4096]{1,0:T(8,128)(2,1)} copy(bf16[512,4096]{1,0:T(8,128)(2,1)} %all-reduce.2.cloned.1.call-done) | data formatting | bytes 8388608
  (8 shorter events, 0.1 us)
Async XLA Ops:
  6.5 37.2 %copy-start.1 = (s32[16,1,1024]{2,1,0:T(1,128)S(1)}, s32[16,1,1024]{2,1,0:T(1,128)}, u32[]{:S(2)}) copy-start(s32[16,1,1024]{2,1,0:T(1,128)} %param.13) | copy-start | bytes 196612
  6.5 53.9 %all-gather.7.cloned.1.call-start = ((), (), s32[]{:S(2)}) async-start(), calls=%async_computation.1 | async-start | bytes 1179648 | tf_op jit(solution)/shard_map/all_gather | solution.py:93
  7.3 58.3 %all-gather.5.cloned.1.call-start = ((), (), s32[]{:S(2)}) async-start(), calls=%async_computation | async-start | bytes 1179648 | tf_op jit(solution)/shard_map/all_gather | solution.py:99
  8.0 109.9 %all-gather.9.cloned.1.call-start = ((), (), s32[]{:S(2)}) async-start(), calls=%async_computation.2 | async-start | bytes 9437184 | tf_op jit(solution)/shard_map/all_gather | solution.py:87
  8.7 166.8 %all-gather.11.cloned.1.call-start = ((), (), s32[]{:S(2)}) async-start(), calls=%async_computation.3 | async-start | bytes 9437184 | tf_op jit(solution)/shard_map/all_gather | solution.py:105
  9.3 338.0 %all-reduce.2.cloned.1.call-start = ((), (), s32[]{:S(2)}) async-start(), calls=%async_computation.4 | async-start | bytes 8388608 | tf_op jit(solution)/shard_map/psum | solution.py:109
  9.4 47.4 %copy-start = (bf16[512,4096]{1,0:T(8,128)(2,1)S(1)}, bf16[512,4096]{1,0:T(8,128)(2,1)}, u32[]{:S(2)}) copy-start(bf16[512,4096]{1,0:T(8,128)(2,1)} %param.10) | copy-start | bytes 12582916
Sparse Core Ops, SparseCore 0:
  9.2 26.8 all-gather.6
  38.0 23.6 all-gather.4
  63.6 54.2 all-gather.8
  119.6 55.8 all-gather.10
  192.3 154.9 all-reduce.1
where the time goes:
time: 359 us
  waiting for transfers between devices  231 us (64%)
  blocking collectives  39.2 us (11%)
  other arithmetic  29.8 us (8%)
  matrix products  26.9 us (7%)
  local copies, waits for them, and re-layouts  17.9 us (5%)
  between operations  13.3 us (4%)
    psum x1, waiting for transfers between devices, shards(): return lax.psum(block_out.astype(jnp.bfloat16), 'tensor')  155 us
    all_gather x1, waiting for transfers between devices, shards(): lax.all_gather(query_blocks, 'dp', axis=0, tiled=True)  47.6 us
    all_gather x1, waiting for transfers between devices, shards(): lax.all_gather(output_blocks, 'dp', axis=2, tiled=True)  26 us
    mul x7, other arithmetic, dequant(): weight = blocks * factor  17.3 us
    dot_general x3, matrix products, product(): jnp.dot(normed, dequant(blocks, scales), preferred_element_type=jnp.float32)  15.4 us
    all_gather x1, blocking collectives, shards(): lax.all_gather(output_exps, 'dp', axis=2, tiled=True)  12.4 us
    dot_general x1, local copies, waits for them, and re-layouts, product(): jnp.dot(normed, dequant(blocks, scales), preferred_element_type=jnp.float32)  12.1 us
    all_gather x1, blocking collectives, shards(): lax.all_gather(query_exps, 'dp', axis=0, tiled=True)  9.4 us
  transfers between devices with their start and end apart: 5, of which 3 were waited for; matrix products, arithmetic and copies ran while one was open for 15% of the time, Pallas kernels for 0%

commit v1 on v0

--- a/solution.py
+++ b/solution.py
@@ -102,7 +102,9 @@
     )
     context = attend(query_states, key_states, value_states, key_blocks.shape[2] // HEAD_DIM)
     pieces = (
-        lax.all_gather(output_blocks, "dp", axis=2, tiled=True),
+        jnp.concatenate(
+            lax.all_to_all(jnp.stack([output_blocks] * lax.axis_size("dp")), "dp", 0, 0), axis=2
+        ),
         lax.all_gather(output_exps, "dp", axis=2, tiled=True),
     )
     block_out = jnp.dot(context, dequant(pieces[0], pieces[1]), preferred_element_type=jnp.float32)

time: 359 us -> 417 us (1.16)
  blocking collectives: 39.2 us -> 134 us
  waiting for transfers between devices: 231 us -> 159 us
  local copies, waits for them, and re-layouts: 17.9 us -> 50.1 us
  starting transfers between devices: 0.15 us -> 5.46 us
    all_gather x1, blocking collectives: 12.4 us -> 106 us  [shards(): lax.all_gather(output_exps, 'dp', axis=2, tiled=True)]
    all_gather x1, waiting for transfers between devices: 47.6 us -> 0.01 us  [shards(): lax.all_gather(query_blocks, 'dp', axis=0, tiled=True)]
    all_gather x1 -> x0, waiting for transfers between devices: 26 us -> none  [shards(): lax.all_gather(output_blocks, 'dp', axis=2, tiled=True)]
    mul x0 -> x2, local copies, waits for them, and re-layouts: none -> 15.6 us  [dequant(): weight = blocks * factor]
    unnamed x6 -> x14, local copies, waits for them, and re-layouts: 5 us -> 16.9 us
    another operation x0 -> x1, local copies, waits for them, and re-layouts: none -> 5.53 us  [shards(): jnp.stack([output_blocks] * lax.axis_size('dp'))]
    all_to_all x0 -> x1, starting transfers between devices: none -> 5.34 us  [shards(): lax.all_to_all(jnp.stack([output_blocks] * lax.axis_size('dp')), 'dp', 0, 0)]
  transfers between devices with their start and end apart: 5 -> 5, of which waited for: 3 -> 1; matrix products, arithmetic and copies ran while one was open for 15% -> 14% of each run, Pallas kernels for 0% -> 0%
where the time goes in v1:
time: 417 us; the launch traced here: 416 us
  waiting for transfers between devices  159 us (38%)
  blocking collectives  134 us (32%)
  local copies, waits for them, and re-layouts  50.1 us (12%)
  other arithmetic  27.4 us (7%)
  matrix products  26.9 us (6%)
  between operations  13.4 us (3%)
  starting transfers between devices  5.46 us (1%)
    psum x1, waiting for transfers between devices, shards(): return lax.psum(block_out.astype(jnp.bfloat16), 'tensor')  157 us
    all_gather x1, blocking collectives, shards(): lax.all_gather(output_exps, 'dp', axis=2, tiled=True)  106 us
    mul x7, other arithmetic, dequant(): weight = blocks * factor  17.2 us
    unnamed x14, local copies, waits for them, and re-layouts  16.9 us
    mul x2, local copies, waits for them, and re-layouts, dequant(): weight = blocks * factor  15.6 us
    dot_general x3, matrix products, product(): jnp.dot(normed, dequant(blocks, scales), preferred_element_type=jnp.float32)  15.4 us
    dot_general x1, local copies, waits for them, and re-layouts, product(): jnp.dot(normed, dequant(blocks, scales), preferred_element_type=jnp.float32)  11.3 us
    all_gather x1, blocking collectives, shards(): lax.all_gather(query_exps, 'dp', axis=0, tiled=True)  9.97 us
  transfers between devices with their start and end apart: 5, of which 1 were waited for; matrix products, arithmetic and copies ran while one was open for 14% of the time, Pallas kernels for 0%

profile of v1, /device:TPU:0, one launch (start us, length us, event | category | flops | bytes accessed | tf_op | source)
XLA Modules:
  0.0 416.1 jit_solution(4603112732686308012)
XLA Ops:
  6.5 0.0 all-gather.6.cloned.1.call-start
  6.5 0.7 all-gather.6.cloned.1.call-update
  7.3 0.0 all-gather.4.cloned.1.call-start
  7.3 0.7 all-gather.4.cloned.1.call-update
  8.0 0.0 all-gather.8.cloned.1.call-start
  8.1 0.7 all-gather.8.cloned.1.call-update
  8.7 5.5 %stack.2 = bf16[8,32,32,512]{3,2,1,0:T(8,128)(2,1)} broadcast(bf16[32,32,512]{2,1,0:T(8,128)(2,1)} %param.18), dimensions={1,2,3} | broadcast | bytes 9437184 | tf_op jit(solution)/shard_map/stack | solution.py:106
  14.3 0.0 copy-start.4
  14.3 0.0 copy-start.5
  14.3 0.0 copy-start.3
  14.3 0.0 copy-start.2
  14.3 0.0 copy-start.1
  14.3 5.3 %all-to-all-start = ((bf16[8,32,32,512]{3,2,1,0:T(8,128)(2,1)}), bf16[8,32,32,512]{3,2,1,0:T(8,128)(2,1)}, u32[]{:S(2)}, u32[]{:S(2)}) async-start(bf16[8,32,32,512]{3,2,1,0:T(8,128)(2,1)} %stack.2), calls=%async_computation | async-start | bytes 16777216 | tf_op jit(solution)/shard_map/all_to_all | solution.py:106
  19.6 0.0 all-reduce.2.cloned.1.call-start
  19.7 0.0 copy-start
  19.7 0.0 copy-done.4
  19.7 0.0 copy-done.5
  19.7 0.0 copy-done.3
  19.8 0.0 copy-done.2
  19.8 106.0 %all_gather.27 = bf16[32,1,4096]{2,1,0:T(2,128)(2,1)S(1)} all-gather(bf16[32,1,512]{2,1,0:T(2,128)(2,1)S(1)} %convert_element_type.110), channel_id=1, replica_groups=mesh['dp'=8,'tensor'=4] {'dp'}, dimensions={2}, use_global_device_ids=true | all-gather | bytes 294912 | tf_op jit(solution)/shard_map/all_gather | solution.py:108
  125.9 1.8 convert_reduce_fusion
  127.7 8.9 %all_gather.22 = bf16[128,1,128]{2,0,1:T(8,128)(2,1)S(1)} all-gather(bf16[16,1,128]{2,0,1:T(8,128)(2,1)S(1)} %convert_element_type.95), channel_id=1, replica_groups=mesh['dp'=8,'tensor'=4] {'dp'}, dimensions={0}, use_global_device_ids=true | all-gather | bytes 36864 | tf_op jit(solution)/shard_map/all_gather | solution.py:100
  136.6 8.7 %all_gather.24 = bf16[128,1,128]{2,0,1:T(8,128)(2,1)S(1)} all-gather(bf16[16,1,128]{2,0,1:T(8,128)(2,1)S(1)} %convert_element_type.99), channel_id=1, replica_groups=mesh['dp'=8,'tensor'=4] {'dp'}, dimensions={0}, use_global_device_ids=true | all-gather | bytes 36864 | tf_op jit(solution)/shard_map/all_gather | solution.py:94
  145.3 0.0 copy-done.1
  145.4 10.0 %all_gather.26 = bf16[128,1,1024]{2,0,1:T(8,128)(2,1)S(1)} all-gather(bf16[16,1,1024]{2,0,1:T(8,128)(2,1)S(1)} %copy_convert_fusion), channel_id=1, replica_groups=mesh['dp'=8,'tensor'=4] {'dp'}, dimensions={0}, use_global_device_ids=true | all-gather | bytes 294912 | tf_op jit(solution)/shard_map/all_gather | solution.py:88
  155.4 3.1 fusion
  158.5 0.3 multiply_cosine_fusion
  158.8 0.1 fusion.20
  158.9 0.0 copy-done
  158.9 3.6 fusion.2
  162.6 0.0 all-gather.6.cloned.1.call-done
  162.6 1.3 broadcast_multiply_fusion.1
  163.9 3.7 convolution_bitcast_fusion
  167.6 0.0 all-gather.4.cloned.1.call-done
  167.7 1.3 broadcast_multiply_fusion.2
  169.0 3.4 convolution_convert_fusion.1
  172.4 0.0 all-to-all-done
  172.4 7.2 %bitcast_multiply_fusion = bf16[32,32,8,512]{3,1,0,2:T(8,128)(2,1)} fusion(bf16[8,32,32,512]{3,2,1,0:T(8,128)(2,1)} %all-to-all-done, bf16[32,8,512]{2,0,1:T(8,128)(2,1)S(1)} %bitcast.99), kind=kLoop, calls=%fused_computation.5 | loop fusion | flops 4194304 | bytes 17039360 | tf_op jit(solution)/shard_map/mul | solution.py:15
  179.7 15.6 %copy.36 = bf16[32,32,8,512]{3,2,1,0:T(8,128)(2,1)} copy(bf16[32,32,8,512]{3,1,0,2:T(8,128)(2,1)} %bitcast_multiply_fusion) | data formatting | bytes 16777216 | tf_op jit(solution)/shard_map/mul | solution.py:15
  195.3 12.2 %copy.50 = bf16[128,8,8,512]{3,1,2,0:T(8,128)(2,1)} copy(bf16[128,8,8,512]{3,2,1,0:T(8,128)(2,1)} %bitcast.93) | data formatting | bytes 16777216
  207.5 0.0 all-gather.8.cloned.1.call-done
  207.5 7.2 %broadcast_multiply_fusion = bf16[128,32,1024]{2,1,0:T(8,128)(2,1)} fusion(bf16[128,32,1024]{2,1,0:T(8,128)(2,1)} %all-gather.8.cloned.1.call-done, bf16[128,1024]{1,0:T(8,128)(2,1)S(1)} %fusion.20), kind=kLoop, calls=%fused_computation.10 | loop fusion | flops 4194304 | bytes 17039360 | tf_op jit(solution)/shard_map/mul | solution.py:15
  214.7 11.3 %copy.29 = bf16[1024,4096]{1,0:T(8,128)(2,1)} copy(bf16[1024,4096]{0,1:T(8,128)(2,1)} %bitcast.92) | data formatting | bytes 16777216 | tf_op jit(solution)/shard_map/dot_general | solution.py:80
  226.0 8.2 %fusion.30 = f32[2,256,8,128]{1,3,2,0:T(8,128)S(1)} fusion(bf16[2,256,4096,1]{2,1,3,0:T(8,128)(2,1)} %bitcast.95, bf16[8,128,4096,1]{2,1,0,3:T(8,128)(2,1)} %bitcast.97), kind=kOutput, calls=%fused_computation.55 | convolution fusion | flops 4294967296 | bytes 14680064 | tf_op jit(solution)/shard_map/dot_general | solution.py:80
  234.2 0.3 subtract_convert_fusion
  234.6 0.8 fusion.4
  235.4 0.9 fusion.3
  236.3 1.3 fusion.11
  237.6 0.8 copy.34
  238.3 9.4 %convolution_convert_fusion = bf16[512,4096]{1,0:T(8,128)(2,1)} fusion(bf16[1024,4096]{1,0:T(8,128)(2,1)} %bitcast.96, bf16[64,8,8,128]{3,2,1,0:T(8,128)(2,1)S(1)} %bitcast.102), kind=kOutput, calls=%fused_computation.6 | convolution fusion | flops 4297064448 | bytes 13631488 | tf_op jit(solution)/shard_map/dot_general | solution.py:110
  247.8 0.0 all-reduce.2.cloned.1.call-update
  247.8 157.1 %all-reduce.2.cloned.1.call-done = bf16[512,4096]{1,0:T(8,128)(2,1)} async-done(((bf16[512,4096]{1,0:T(8,128)(2,1)}), bf16[512,4096]{1,0:T(8,128)(2,1)}) %all-reduce.2.cloned.1.call-update) | async-done | bytes 4194320 | tf_op jit(solution)/shard_map/psum | solution.py:111
  404.8 4.7 %copy.59 = bf16[512,4096]{1,0:T(8,128)(2,1)} copy(bf16[512,4096]{1,0:T(8,128)(2,1)} %all-reduce.2.cloned.1.call-done) | data formatting | bytes 8388608
  (13 shorter events, 0.2 us)
Async XLA Ops:
  6.5 156.0 %all-gather.6.cloned.1.call-start = ((), (), s32[]{:S(2)}) async-start(), calls=%async_computation.2 | async-start | bytes 1179648 | tf_op jit(solution)/shard_map/all_gather | solution.py:93
  7.3 160.4 %all-gather.4.cloned.1.call-start = ((), (), s32[]{:S(2)}) async-start(), calls=%async_computation.1 | async-start | bytes 1179648 | tf_op jit(solution)/shard_map/all_gather | solution.py:99
  8.0 199.5 %all-gather.8.cloned.1.call-start = ((), (), s32[]{:S(2)}) async-start(), calls=%async_computation.3 | async-start | bytes 9437184 | tf_op jit(solution)/shard_map/all_gather | solution.py:87
  14.3 5.4 %copy-start.4 = (s32[16,1,128]{2,1,0:T(1,128)S(1)}, s32[16,1,128]{2,1,0:T(1,128)}, u32[]{:S(2)}) copy-start(s32[16,1,128]{2,1,0:T(1,128)} %param.15) | copy-start | bytes 24580
  14.3 5.4 %copy-start.5 = (s32[16,1,128]{2,1,0:T(1,128)S(1)}, s32[16,1,128]{2,1,0:T(1,128)}, u32[]{:S(2)}) copy-start(s32[16,1,128]{2,1,0:T(1,128)} %param.17) | copy-start | bytes 24580
  14.3 5.5 %copy-start.3 = (bf16[4096]{0:T(1024)(128)(2,1)S(1)}, bf16[4096]{0:T(1024)(128)(2,1)}, u32[]{:S(2)}) copy-start(bf16[4096]{0:T(1024)(128)(2,1)} %param.11) | copy-start | bytes 24580
  14.3 5.5 %copy-start.2 = (s32[32,1,512]{2,1,0:T(1,128)S(1)}, s32[32,1,512]{2,1,0:T(1,128)}, u32[]{:S(2)}) copy-start(s32[32,1,512]{2,1,0:T(1,128)} %param.19) | copy-start | bytes 196612
  14.3 131.1 %copy-start.1 = (s32[16,1,1024]{2,1,0:T(1,128)S(1)}, s32[16,1,1024]{2,1,0:T(1,128)}, u32[]{:S(2)}) copy-start(s32[16,1,1024]{2,1,0:T(1,128)} %param.13) | copy-start | bytes 196612
  14.3 158.1 %all-to-all-start = ((bf16[8,32,32,512]{3,2,1,0:T(8,128)(2,1)}), bf16[8,32,32,512]{3,2,1,0:T(8,128)(2,1)}, u32[]{:S(2)}, u32[]{:S(2)}) async-start(bf16[8,32,32,512]{3,2,1,0:T(8,128)(2,1)} %stack.2), calls=%async_computation | async-start | bytes 16777216 | tf_op jit(solution)/shard_map/all_to_all | solution.py:106
  19.6 385.2 %all-reduce.2.cloned.1.call-start = ((), (), s32[]{:S(2)}) async-start(), calls=%async_computation.4 | async-start | bytes 8388608 | tf_op jit(solution)/shard_map/psum | solution.py:111
  19.7 139.3 %copy-start = (bf16[512,4096]{1,0:T(8,128)(2,1)S(1)}, bf16[512,4096]{1,0:T(8,128)(2,1)}, u32[]{:S(2)}) copy-start(bf16[512,4096]{1,0:T(8,128)(2,1)} %param.10) | copy-start | bytes 12582916
Sparse Core Ops, SparseCore 0:
  9.2 67.1 all-gather.5
  78.3 34.8 all-gather.3
  115.1 54.9 all-gather.7
  247.9 156.8 all-reduce.1
